TPU v7x, 32 devices: a whole 2x2x4 slice. The times are simulated.
32 devices in a mesh: dp: 4 (over y, x), expert: 8 (over z, core).
Axes of the slice: x: 2, y: 2, z: 4, core: 2. Of those that a mesh axis runs over, the one named last changes fastest.
Arguments:
- tokens: bfloat16 [8192, 1024], P(('dp', 'expert')), may hold values from -6 to 6
- segment_ids: int32 [8192], P(('dp', 'expert')), may hold values from 0 to 12, as said below
- parent_ids: int32 [8192], P(('dp', 'expert')), may hold values from 0 to 10, as said below
- path_depth: int32 [8192], P(('dp', 'expert')), may hold values from 0 to 245, as said below
- routes: int32 [8192, 2], P(('dp', 'expert')), may hold values from 0 to 15, as said below
- slot_index: int32 [8192, 2], P(('dp', 'expert')), may hold values from 0 to 39, as said below
- gain_attn: bfloat16 [1024], P('dp'), may hold values from 0.5 to 1.5
- w_query: bfloat16 [1024, 1024], P('dp'), may hold values from -0.25 to 0.25
- w_key: bfloat16 [1024, 1024], P('dp'), may hold values from -0.25 to 0.25
- w_value: bfloat16 [1024, 1024], P('dp'), may hold values from -0.1875 to 0.1875
- w_out: bfloat16 [1024, 1024], P('dp'), may hold values from -0.75 to 0.75
- gain_moe: bfloat16 [1024], P('dp'), may hold values from 0.5 to 1.5
- w_router: bfloat16 [1024, 16], P('dp'), may hold values from -0.09375 to 0.09375
- w_gate: bfloat16 [16, 1024, 2816], P('expert', None, 'dp'), may hold values from -0.1875 to 0.1875
- w_up: bfloat16 [16, 1024, 2816], P('expert', None, 'dp'), may hold values from -0.1875 to 0.1875
- w_down: bfloat16 [16, 2816, 1024], P('expert', 'dp'), may hold values from -0.21875 to 0.21875
- cotangent: bfloat16 [8192, 1024], P(('dp', 'expert')), may hold values from -6 to 6
Outputs:
- output: bfloat16 [8192, 1024], P(('dp', 'expert'))
- token_grad: float32 [8192, 1024], P(('dp', 'expert'))
- gain_attn_grad: float32 [1024], P(('dp', 'expert'))
- query_grad: float32 [1024, 1024], P(('dp', 'expert'))
- key_grad: float32 [1024, 1024], P(('dp', 'expert'))
- value_grad: float32 [1024, 1024], P(('dp', 'expert'))
- out_proj_grad: float32 [1024, 1024], P(('dp', 'expert'))
- gain_moe_grad: float32 [1024], P(('dp', 'expert'))
- router_grad: float32 [1024, 16], P(('dp', 'expert'))
- gate_grad: float32 [16, 1024, 2816], P('expert', None, 'dp')
- up_grad: float32 [16, 1024, 2816], P('expert', None, 'dp')
- down_grad: float32 [16, 2816, 1024], P('expert', 'dp')
Inputs may be any that keep to these rules, and one draw needn't show every extreme that they name: `segment_ids`: in each aligned block of 256 tokens (one tree sequence) segment ids never fall; 0 is the trunk, 1, 4, 7 and 10 are branches, each followed by its two leaves; every segment has one token or more. `parent_ids`: the id of the parent of the token's segment; 0 for the trunk and the branches. `path_depth`: trunk tokens count from 0, a branch continues after the trunk, a leaf after its branch; the bound is reached in some sequence. `routes`: a token's two experts differ; within the rows of one device each expert is named by at most 40 tokens, and one expert, the same on every device, by exactly 40. `slot_index`: within the rows of one device, pairs routed to the same expert have different slots.
All inputs are finite; a program needn't handle non-finite values.
Results may differ from a plain program's by a relative error of at most 0.015.
The roundings to bfloat16 on the way count: a program that leaves them out, or rounds other values in their place, can miss the bound.
Values may be sent and summed in bfloat16 or wider, within the bound.
A program may use at most 256 MiB of HBM per device.

v0:
```python
import jax
import jax.numpy as jnp
from jax import lax
from jax.sharding import PartitionSpec as P

HEADS = 16
HEAD_DIM = 64
EXPERTS = 16
CAP = 40


EPS = 1e-06


def rms_scale(values, gain_vec):
    return values * lax.rsqrt(jnp.mean(values * values, axis=-1, keepdims=True) + EPS) * gain_vec


def rotate(values, cosine_part, sine_part):
    half_dim = values.shape[-1] // 2
    leading = values[..., :half_dim]
    trailing = values[..., half_dim:]
    return jnp.concatenate(
        [
            leading * cosine_part - trailing * sine_part,
            leading * sine_part + trailing * cosine_part,
        ],
        axis=-1,
    )


def angles(path_depth):
    half_dim = HEAD_DIM // 2
    frequency = 10000.0 ** (-jnp.arange(half_dim, dtype=jnp.float32) * 2.0 / HEAD_DIM)
    turned = path_depth.astype(jnp.float32)[:, None] * frequency[None, :]
    return (jnp.cos(turned)[:, None, :], jnp.sin(turned)[:, None, :])


def visible(segment, parent):
    position = jnp.arange(segment.shape[0])
    causal = position[None, :] <= position[:, None]
    related = (
        (segment[None, :] == segment[:, None])
        | (segment[None, :] == parent[:, None])
        | (segment[None, :] == 0)
    )
    return causal & related


def glu_apply(gate_part, up_part):
    return jax.nn.gelu(gate_part, approximate=True) * up_part


def shards(
    tokens,
    segment_ids,
    parent_ids,
    path_depth,
    routes,
    slot_index,
    gain_attn,
    w_query,
    w_key,
    w_value,
    w_out,
    gain_moe,
    w_router,
    w_gate,
    w_up,
    w_down,
    cotangent,
):
    token_count = tokens.shape[0]
    model_width = tokens.shape[1]
    gain_one, query_w, key_w, value_w, out_w, gain_two, router_w = (
        lax.all_gather(gain_attn, "dp", axis=0, tiled=True),
        lax.all_gather(w_query, "dp", axis=0, tiled=True),
        lax.all_gather(w_key, "dp", axis=0, tiled=True),
        lax.all_gather(w_value, "dp", axis=0, tiled=True),
        lax.all_gather(w_out, "dp", axis=0, tiled=True),
        lax.all_gather(gain_moe, "dp", axis=0, tiled=True),
        lax.all_gather(w_router, "dp", axis=0, tiled=True),
    )
    gate_w, up_w, down_w = (w_gate, w_up, w_down)
    inputs = tokens.astype(jnp.float32)
    gain_onef = gain_one.astype(jnp.float32)
    gain_twof = gain_two.astype(jnp.float32)
    normed = rms_scale(inputs, gain_onef).astype(jnp.bfloat16)
    queries = jnp.dot(normed, query_w, preferred_element_type=jnp.float32).reshape(
        token_count, HEADS, HEAD_DIM
    )
    keys_all = jnp.dot(normed, key_w, preferred_element_type=jnp.float32).reshape(
        token_count, HEADS, HEAD_DIM
    )
    values_low = (
        jnp.dot(normed, value_w, preferred_element_type=jnp.float32)
        .astype(jnp.bfloat16)
        .reshape(token_count, HEADS, HEAD_DIM)
    )
    cosine_part, sine_part = angles(path_depth)
    queries_low = (rotate(queries, cosine_part, sine_part) * 0.125).astype(jnp.bfloat16)
    keys_low = rotate(keys_all, cosine_part, sine_part).astype(jnp.bfloat16)
    allowed = visible(segment_ids, parent_ids)[None]
    scores = jnp.einsum("qhd,khd->hqk", queries_low, keys_low, preferred_element_type=jnp.float32)
    scores = jnp.where(allowed, scores, -1e30)
    row_top = jnp.max(scores, axis=-1, keepdims=True)
    exponent = jnp.exp(scores - row_top)
    totals = jnp.sum(exponent, axis=-1, keepdims=True)
    log_total = row_top + jnp.log(totals)
    softmaxed = exponent / totals
    attn_mixed = jnp.einsum(
        "hqk,khd->qhd",
        softmaxed.astype(jnp.bfloat16),
        values_low,
        preferred_element_type=jnp.float32,
    )
    attn_mixed = attn_mixed.reshape(token_count, model_width).astype(jnp.bfloat16)
    residual = inputs + jnp.dot(attn_mixed, out_w, preferred_element_type=jnp.float32)
    routed_in = rms_scale(residual, gain_twof).astype(jnp.bfloat16)
    logits = jnp.dot(routed_in, router_w, preferred_element_type=jnp.float32)
    picker = (routes[:, :, None] == jnp.arange(EXPERTS)[None, None, :]).astype(jnp.float32)
    chosen = jnp.sum(picker * logits[:, None, :], axis=2)
    gate_values = jax.nn.softmax(chosen, axis=1)
    flat_slot = routes * CAP + slot_index
    owners = (
        jnp.zeros((EXPERTS * CAP,), jnp.int32)
        .at[flat_slot.reshape(-1)]
        .set(jnp.arange(2 * token_count, dtype=jnp.int32) + 1)
    )
    source_row = jnp.where(owners > 0, (owners - 1) // 2 + 1, 0)
    padded_in = jnp.concatenate([jnp.zeros((1, model_width), jnp.bfloat16), routed_in], axis=0)
    outgoing = padded_in[source_row].reshape(EXPERTS, CAP, model_width)
    arrived = lax.all_to_all(outgoing, "expert", split_axis=0, concat_axis=1, tiled=True)
    rows_used = lax.all_gather(arrived, "dp", axis=1, tiled=True)
    gate_pre = jnp.einsum("erd,edf->erf", rows_used, gate_w, preferred_element_type=jnp.float32)
    up_pre = jnp.einsum("erd,edf->erf", rows_used, up_w, preferred_element_type=jnp.float32)
    hidden = glu_apply(gate_pre, up_pre).astype(jnp.bfloat16)
    produced_terms = jnp.einsum("erf,efd->erd", hidden, down_w, preferred_element_type=jnp.float32)
    produced = lax.psum_scatter(
        produced_terms.astype(jnp.bfloat16), "dp", scatter_dimension=1, tiled=True
    )
    came_back = lax.all_to_all(produced, "expert", split_axis=1, concat_axis=0, tiled=True).reshape(
        EXPERTS * CAP, model_width
    )
    returned = came_back[flat_slot].astype(jnp.float32)
    moe_out = jnp.sum(gate_values[:, :, None] * returned, axis=1)
    output = (residual + moe_out).astype(jnp.bfloat16)
    upstream = cotangent.astype(jnp.float32)
    gate_value_grad = jnp.sum(upstream[:, None, :] * returned, axis=2)
    chosen_grad = gate_values * (
        gate_value_grad - jnp.sum(gate_values * gate_value_grad, axis=1, keepdims=True)
    )
    logit_grad = jnp.sum(picker * chosen_grad[:, :, None], axis=1).astype(jnp.bfloat16)
    pair_grad = (
        (gate_values[:, :, None] * upstream[:, None, :])
        .astype(jnp.bfloat16)
        .reshape(2 * token_count, model_width)
    )
    padded_grad = jnp.concatenate([jnp.zeros((1, model_width), jnp.bfloat16), pair_grad], axis=0)
    outgoing_grad = padded_grad[owners].reshape(EXPERTS, CAP, model_width)
    arrived_grad = lax.all_to_all(outgoing_grad, "expert", split_axis=0, concat_axis=1, tiled=True)
    grads_used = lax.all_gather(arrived_grad, "dp", axis=1, tiled=True)
    gate_back, up_back, down_back = (w_gate, w_up, w_down)
    hidden_grad = jnp.einsum(
        "erd,efd->erf", grads_used, down_back, preferred_element_type=jnp.float32
    )
    down_wgrad = jnp.einsum("erf,erd->efd", hidden, grads_used, preferred_element_type=jnp.float32)
    unused_value, glu_pull = jax.vjp(glu_apply, gate_pre, up_pre)
    gate_pre_grad, up_pre_grad = glu_pull(hidden_grad)
    gate_low = gate_pre_grad.astype(jnp.bfloat16)
    up_low = up_pre_grad.astype(jnp.bfloat16)
    gate_wgrad = jnp.einsum("erd,erf->edf", rows_used, gate_low, preferred_element_type=jnp.float32)
    up_wgrad = jnp.einsum("erd,erf->edf", rows_used, up_low, preferred_element_type=jnp.float32)
    rows_terms = jnp.einsum("erf,edf->erd", gate_low, gate_back, preferred_element_type=jnp.float32)
    rows_terms = rows_terms + jnp.einsum(
        "erf,edf->erd", up_low, up_back, preferred_element_type=jnp.float32
    )
    gate_sum, up_sum, down_sum = (gate_wgrad, up_wgrad, down_wgrad)
    rows_grad = lax.psum_scatter(
        rows_terms.astype(jnp.bfloat16), "dp", scatter_dimension=1, tiled=True
    )
    sent_back = lax.all_to_all(
        rows_grad, "expert", split_axis=1, concat_axis=0, tiled=True
    ).reshape(EXPERTS * CAP, model_width)
    query_back, key_back, value_back, out_back, router_back = (
        query_w,
        key_w,
        value_w,
        out_w,
        router_w,
    )
    routed_grad = jnp.sum(sent_back[flat_slot].astype(jnp.float32), axis=1)
    routed_grad = routed_grad + jnp.dot(
        logit_grad, router_back.T, preferred_element_type=jnp.float32
    )
    router_wgrad = jnp.einsum(
        "td,te->de", routed_in, logit_grad, preferred_element_type=jnp.float32
    )
    unused_norm, second_pull = jax.vjp(rms_scale, residual, gain_twof)
    residual_norm_grad, gain_two_grad = second_pull(routed_grad)
    residual_grad = upstream + residual_norm_grad
    branch_grad = residual_grad.astype(jnp.bfloat16)
    out_wgrad = jnp.einsum("td,te->de", attn_mixed, branch_grad, preferred_element_type=jnp.float32)
    mixed_grad = (
        jnp.dot(branch_grad, out_back.T, preferred_element_type=jnp.float32)
        .astype(jnp.bfloat16)
        .reshape(token_count, HEADS, HEAD_DIM)
    )
    scores = jnp.einsum("qhd,khd->hqk", queries_low, keys_low, preferred_element_type=jnp.float32)
    scores = jnp.where(allowed, scores, -1e30)
    softmaxed = jnp.exp(scores - log_total)
    value_low_grad = jnp.einsum(
        "hqk,qhd->khd",
        softmaxed.astype(jnp.bfloat16),
        mixed_grad,
        preferred_element_type=jnp.float32,
    )
    value_low_grad = value_low_grad.reshape(token_count, model_width).astype(jnp.bfloat16)
    weight_grad = jnp.einsum(
        "qhd,khd->hqk", mixed_grad, values_low, preferred_element_type=jnp.float32
    )
    score_grad = (
        softmaxed * (weight_grad - jnp.sum(softmaxed * weight_grad, axis=-1, keepdims=True))
    ).astype(jnp.bfloat16)
    query_rot_grad = (
        jnp.einsum("hqk,khd->qhd", score_grad, keys_low, preferred_element_type=jnp.float32) * 0.125
    )
    key_rot_grad = jnp.einsum(
        "hqk,qhd->khd", score_grad, queries_low, preferred_element_type=jnp.float32
    )
    query_low_grad = (
        rotate(query_rot_grad, cosine_part, -sine_part)
        .reshape(token_count, model_width)
        .astype(jnp.bfloat16)
    )
    key_low_grad = (
        rotate(key_rot_grad, cosine_part, -sine_part)
        .reshape(token_count, model_width)
        .astype(jnp.bfloat16)
    )
    query_wgrad = jnp.einsum(
        "td,te->de", normed, query_low_grad, preferred_element_type=jnp.float32
    )
    key_wgrad = jnp.einsum("td,te->de", normed, key_low_grad, preferred_element_type=jnp.float32)
    value_wgrad = jnp.einsum(
        "td,te->de", normed, value_low_grad, preferred_element_type=jnp.float32
    )
    normed_grad = jnp.dot(query_low_grad, query_back.T, preferred_element_type=jnp.float32)
    normed_grad = normed_grad + jnp.dot(
        key_low_grad, key_back.T, preferred_element_type=jnp.float32
    )
    normed_grad = normed_grad + jnp.dot(
        value_low_grad, value_back.T, preferred_element_type=jnp.float32
    )
    unused_first, first_pull = jax.vjp(rms_scale, inputs, gain_onef)
    input_norm_grad, gain_one_grad = first_pull(normed_grad)
    token_grad = residual_grad + input_norm_grad
    summed = (
        lax.psum_scatter(gain_one_grad, ("dp", "expert"), scatter_dimension=0, tiled=True),
        lax.psum_scatter(query_wgrad, ("dp", "expert"), scatter_dimension=0, tiled=True),
        lax.psum_scatter(key_wgrad, ("dp", "expert"), scatter_dimension=0, tiled=True),
        lax.psum_scatter(value_wgrad, ("dp", "expert"), scatter_dimension=0, tiled=True),
        lax.psum_scatter(out_wgrad, ("dp", "expert"), scatter_dimension=0, tiled=True),
        lax.psum_scatter(gain_two_grad, ("dp", "expert"), scatter_dimension=0, tiled=True),
        lax.psum_scatter(router_wgrad, ("dp", "expert"), scatter_dimension=0, tiled=True),
    )
    return (
        output,
        token_grad,
        summed[0],
        summed[1],
        summed[2],
        summed[3],
        summed[4],
        summed[5],
        summed[6],
        gate_sum,
        up_sum,
        down_sum,
    )


def solution(mesh):
    in_specs = (
        P(("dp", "expert"), None),
        P(("dp", "expert")),
        P(("dp", "expert")),
        P(("dp", "expert")),
        P(("dp", "expert"), None),
        P(("dp", "expert"), None),
        P("dp"),
        P("dp", None),
        P("dp", None),
        P("dp", None),
        P("dp", None),
        P("dp"),
        P("dp", None),
        P("expert", None, "dp"),
        P("expert", None, "dp"),
        P("expert", "dp", None),
        P(("dp", "expert"), None),
    )
    out_specs = (
        P(("dp", "expert"), None),
        P(("dp", "expert"), None),
        P(("dp", "expert")),
        P(("dp", "expert"), None),
        P(("dp", "expert"), None),
        P(("dp", "expert"), None),
        P(("dp", "expert"), None),
        P(("dp", "expert")),
        P(("dp", "expert"), None),
        P("expert", None, "dp"),
        P("expert", None, "dp"),
        P("expert", "dp", None),
    )
    return jax.shard_map(shards, mesh=mesh, in_specs=in_specs, out_specs=out_specs, check_vma=False)
```

profile of v0, /device:TPU:0, one launch (start us, length us, event | category | flops | bytes accessed | tf_op | source)
XLA Modules:
  0.0 1213.8 jit_solution(14422454933227244590)
XLA Ops:
  15.6 9.5 all-gather.1
  25.2 8.0 all-gather
  34.8 2.6 scatter_custom_fusion
  38.9 1.5 fusion.36
  40.4 7.5 all-gather.9.cloned.1.call-done
  47.9 3.3 convolution_convert_fusion.2
  51.3 2.1 copy.97
  53.3 31.8 %all-gather.11.cloned.1.call-done = bf16[1024,1024]{1,0:T(8,128)(2,1)} async-done(((bf16[256,1024]{1,0:T(8,128)(2,1)}), bf16[1024,1024]{1,0:T(8,128)(2,1)}) %all-gather.11.cloned.1.call-update) | async-done | bytes 2097168 | tf_op jit(solution)/shard_map/all_gather | solution.py:77
  85.1 3.6 fusion.66
  88.7 33.6 %all-gather.13.cloned.1.call-done = bf16[1024,1024]{1,0:T(8,128)(2,1)} async-done(((bf16[256,1024]{1,0:T(8,128)(2,1)}), bf16[1024,1024]{1,0:T(8,128)(2,1)}) %all-gather.13.cloned.1.call-update) | async-done | bytes 2097168 | tf_op jit(solution)/shard_map/all_gather | solution.py:78
  122.3 2.7 fusion.64
  129.8 1.9 fusion.19
  131.7 27.7 %all-gather.15.cloned.1.call-done = bf16[1024,1024]{1,0:T(8,128)(2,1)} async-done(((bf16[256,1024]{1,0:T(8,128)(2,1)}), bf16[1024,1024]{1,0:T(8,128)(2,1)}) %all-gather.15.cloned.1.call-update) | async-done | bytes 2097168 | tf_op jit(solution)/shard_map/all_gather | solution.py:80
  159.4 2.6 multiply_reduce_fusion.5
  164.0 3.5 gather_fusion
  167.5 36.8 %all_to_all.66 = bf16[16,40,1024]{2,1,0:T(8,128)(2,1)S(1)} all-to-all(bf16[16,40,1024]{2,1,0:T(8,128)(2,1)} %bitcast.92), channel_id=1, replica_groups=mesh['dp'=4,'expert'=8] {'expert'}, dimensions={0} | all-to-all | bytes 2621440 | tf_op jit(solution)/shard_map/all_to_all | solution.py:133
  205.6 3.0 mul.414
  208.6 3.6 mul.415
  212.2 8.8 all_gather.33
  224.1 1.6 div.80
  225.7 1.8 multiply_convert_fusion.3
  228.7 5.8 gather_fusion.2
  234.5 35.7 %all_to_all.67 = bf16[16,40,1024]{2,1,0:T(8,128)(2,1)S(1)} all-to-all(bf16[16,40,1024]{2,1,0:T(8,128)(2,1)} %bitcast.93), channel_id=1, replica_groups=mesh['dp'=4,'expert'=8] {'expert'}, dimensions={0} | all-to-all | bytes 2621440 | tf_op jit(solution)/shard_map/all_to_all | solution.py:161
  271.5 10.4 fusion.71
  281.9 5.9 fusion.70
  287.9 43.1 %all-gather.19.cloned.1.call-done = bf16[2,1280,1024]{2,1,0:T(8,128)(2,1)} async-done(((bf16[2,320,1024]{2,1,0:T(8,128)(2,1)}), bf16[2,1280,1024]{2,1,0:T(8,128)(2,1)}) %all-gather.19.cloned.1.call-update) | async-done | bytes 5242896 | tf_op jit(solution)/shard_map/all_gather | solution.py:162
  331.0 15.2 %multiply_convert_fusion = (bf16[2,1280,704]{1,2,0:T(8,128)(2,1)}, bf16[2,1280,704]{1,2,0:T(8,128)(2,1)}, bf16[2,1280,704]{1,2,0:T(8,128)(2,1)S(1)}) fusion(f32[2,1280,704]{1,2,0:T(8,128)} %fusion.70, f32[2,1280,704]{1,2,0:T(8,128)} %fusion.71, bf16[2,1280,1024]{2,1,0:T(8,128)(2,1)} %all-gather.19.cloned.1.call-done, bf16[2,704,1024]{2,1,0:T(8,128)(2,1)S(1)} %copy-done), kind=kOutput, calls=%fused_computation.15 | convolution fusion | flops 3737845760 | bytes 33357824 | tf_op jit(solution)/shard_map/erd,efd->erf/dot_general | solution.py:164
  346.2 1.8 copy-done.64
  348.0 6.0 convolution_convert_fusion
  355.8 9.0 fusion.72
  364.8 8.5 add_convert_fusion
  373.4 42.2 %reduce-scatter.10.cloned.1.call-done = bf16[2,320,1024]{2,1,0:T(8,128)(2,1)} async-done(((bf16[2,1280,1024]{2,1,0:T(8,128)(2,1)}), bf16[2,320,1024]{2,1,0:T(8,128)(2,1)}) %reduce-scatter.10.cloned.1.call-update) | async-done | bytes 1310736 | tf_op jit(solution)/shard_map/reduce_scatter | solution.py:139
  415.6 3.7 copy.104
  419.4 4.7 all-to-all-start.1
  424.1 56.5 %reduce-scatter.12.cloned.1.call-done = bf16[2,320,1024]{2,1,0:T(8,128)(2,1)} async-done(((bf16[2,1280,1024]{2,1,0:T(8,128)(2,1)}), bf16[2,320,1024]{2,1,0:T(8,128)(2,1)}) %reduce-scatter.12.cloned.1.call-update) | async-done | bytes 1310736 | tf_op jit(solution)/shard_map/reduce_scatter | solution.py:179
  480.6 3.7 copy.109
  484.4 4.6 all-to-all-start.3
  491.0 2.8 gather_fusion.1
  493.7 2.4 reshape.446
  496.1 5.9 multiply_reduce_fusion.1
  503.4 18.4 %all-to-all-done.3 = bf16[2,320,1024]{2,0,1:T(2,128)(2,1)} async-done(((bf16[2,320,1024]{2,0,1:T(2,128)(2,1)}), bf16[2,320,1024]{2,0,1:T(2,128)(2,1)}, u32[]{:S(2)}, u32[]{:S(2)}) %all-to-all-start.3) | async-done | bytes 1310752 | tf_op jit(solution)/shard_map/all_to_all | solution.py:182
  521.8 1.7 copy.110
  523.5 2.8 gather_fusion.3
  526.3 3.5 reshape.447
  529.8 4.1 reduce_sum.141
  535.0 2.4 fusion.24
  537.4 2.8 fusion.30
  540.5 2.4 convolution_convert_fusion.1
  543.1 3.1 fusion.16
  546.3 2.8 fusion.58
  549.2 3.7 multiply_reduce_fusion
  556.0 2.8 fusion.60
  559.2 2.8 fusion.62
  562.1 10.1 fusion.74
  572.2 8.4 fusion.76
  580.6 5.7 fusion.75
  588.7 1.9 fusion.23
  590.6 37.0 %all-reduce.4 = (f32[1024]{0:T(1024)S(1)}, f32[1024]{0:T(1024)S(1)}) all-reduce(f32[1024]{0:T(1024)S(1)} %get-tuple-element.16, f32[1024]{0:T(1024)S(1)} %copy-done.45), channel_id=4, replica_groups=mesh['dp'=4,'expert'=8] {'dp','expert'}, use_global_device_ids=true, to_apply=%region_19.20.clone | all-reduce | flops 2048 | bytes 16384
  628.8 2.8 fusion.25
  631.6 6.8 reduce-scatter.22.cloned.1.call-done
  639.8 140.2 %reduce-scatter.20.cloned.1.call-done = f32[32,1024]{1,0:T(8,128)} async-done(((f32[1024,1024]{1,0:T(8,128)}), f32[32,1024]{1,0:T(8,128)}) %reduce-scatter.20.cloned.1.call-update) | async-done | bytes 131088 | tf_op jit(solution)/shard_map/reduce_scatter | solution.py:263
  780.0 142.4 %reduce-scatter.18.cloned.1.call-done = f32[32,1024]{1,0:T(8,128)} async-done(((f32[1024,1024]{1,0:T(8,128)}), f32[32,1024]{1,0:T(8,128)}) %reduce-scatter.18.cloned.1.call-update) | async-done | bytes 131088 | tf_op jit(solution)/shard_map/reduce_scatter | solution.py:262
  922.5 141.9 %reduce-scatter.16.cloned.1.call-done = f32[32,1024]{1,0:T(8,128)} async-done(((f32[1024,1024]{1,0:T(8,128)}), f32[32,1024]{1,0:T(8,128)}) %reduce-scatter.16.cloned.1.call-update) | async-done | bytes 131088 | tf_op jit(solution)/shard_map/reduce_scatter | solution.py:261
  1064.3 142.5 %reduce-scatter.14.cloned.1.call-done = f32[32,1024]{1,0:T(8,128)} async-done(((f32[1024,1024]{1,0:T(8,128)}), f32[32,1024]{1,0:T(8,128)}) %reduce-scatter.14.cloned.1.call-update) | async-done | bytes 131088 | tf_op jit(solution)/shard_map/reduce_scatter | solution.py:260
  (220 shorter events, 40.0 us)
Async XLA Ops:
  7.2 323.8 %copy-start = (bf16[2,704,1024]{2,1,0:T(8,128)(2,1)S(1)}, bf16[2,704,1024]{2,1,0:T(8,128)(2,1)}, u32[]{:S(2)}) copy-start(bf16[2,704,1024]{2,1,0:T(8,128)(2,1)} %param.32) | copy-start | bytes 8650756
  7.2 77.9 %copy-start.4 = (bf16[256,1024]{1,0:T(8,128)(2,1)S(1)}, bf16[256,1024]{1,0:T(8,128)(2,1)}, u32[]{:S(2)}) copy-start(bf16[256,1024]{1,0:T(8,128)(2,1)} %param.17) | copy-start | bytes 1572868
  7.2 40.7 %all-gather.9.cloned.1.call-start = ((), (), s32[]{:S(2)}) async-start(), calls=%async_computation.11 | async-start | bytes 2621440 | tf_op jit(solution)/shard_map/all_gather | solution.py:79
  7.9 77.2 %all-gather.11.cloned.1.call-start = ((), (), s32[]{:S(2)}) async-start(), calls=%async_computation.12 | async-start | bytes 2621440 | tf_op jit(solution)/shard_map/all_gather | solution.py:77
  8.7 113.6 %all-gather.13.cloned.1.call-start = ((), (), s32[]{:S(2)}) async-start(), calls=%async_computation.13 | async-start | bytes 2621440 | tf_op jit(solution)/shard_map/all_gather | solution.py:78
  9.4 149.9 %all-gather.15.cloned.1.call-start = ((), (), s32[]{:S(2)}) async-start(), calls=%async_computation.14 | async-start | bytes 2621440 | tf_op jit(solution)/shard_map/all_gather | solution.py:80
  10.0 261.5 %all-gather.17.cloned.1.call-start = ((), (), s32[]{:S(2)}) async-start(), calls=%async_computation.15 | async-start | bytes 6553600 | tf_op jit(solution)/shard_map/all_gather | solution.py:134
  13.1 109.3 %copy-start.42 = (f32[256]{0:T(256)}, f32[256]{0:T(256)S(1)}, u32[]{:S(2)}) copy-start(f32[256]{0:T(256)S(1)} %fusion.48) | copy-start | bytes 3076
  25.2 136.8 %copy-start.40 = (f32[4,1,256]{2,1,0:T(1,128)}, f32[4,1,256]{2,1,0:T(1,128)S(1)}, u32[]{:S(2)}) copy-start(f32[4,1,256]{2,1,0:T(1,128)S(1)} %convert_element_type.136) | copy-start | bytes 12292
  33.2 89.1 %copy-start.33 = (f32[4,1,256]{2,1,0:T(1,128)}, f32[4,1,256]{2,1,0:T(1,128)S(1)}, u32[]{:S(2)}) copy-start(f32[4,1,256]{2,1,0:T(1,128)S(1)} %convert_element_type.135) | copy-start | bytes 12292
  122.3 2.7 copy-start.23
  126.9 2.9 copy-start.28
  127.7 3.9 copy-start.35
  162.0 5.5 copy-start.53
  162.0 5.5 copy-start.49
  205.5 6.7 copy-start.56
  205.5 15.6 %copy-start.12 = (bf16[256,1024]{1,0:T(8,128)(2,1)S(1)}, bf16[256,1024]{1,0:T(8,128)(2,1)}, u32[]{:S(2)}) copy-start(bf16[256,1024]{1,0:T(8,128)(2,1)} %copy-done.11) | copy-start | bytes 1572868
  205.5 15.8 %copy-start.44 = (s32[256,2]{0,1:T(2,128)S(1)}, s32[256,2]{0,1:T(2,128)}, u32[]{:S(2)}) copy-start(s32[256,2]{0,1:T(2,128)} %param.21) | copy-start | bytes 6148
  205.5 125.5 %all-gather.19.cloned.1.call-start = ((), (), s32[]{:S(2)}) async-start(), calls=%async_computation.17 | async-start | bytes 6553600 | tf_op jit(solution)/shard_map/all_gather | solution.py:162
  208.6 20.2 %copy-start.46 = (s32[1024]{0:T(1024)S(1)}, s32[1024]{0:T(1024)}, u32[]{:S(2)}) copy-start(s32[1024]{0:T(1024)} %get-tuple-element.52) | copy-start | bytes 12292
  271.4 144.2 %reduce-scatter.10.cloned.1.call-start = ((), (), s32[]{:S(2)}) async-start(), calls=%async_computation.16 | async-start | bytes 6553600 | tf_op jit(solution)/shard_map/reduce_scatter | solution.py:139
  271.5 10.4 copy-start.57
  271.5 10.4 copy-start.58
  354.0 126.6 %reduce-scatter.12.cloned.1.call-start = ((), (), s32[]{:S(2)}) async-start(), calls=%async_computation.18 | async-start | bytes 6553600 | tf_op jit(solution)/shard_map/reduce_scatter | solution.py:179
  355.8 9.0 copy-start.60
  355.8 9.0 copy-start.61
  419.4 69.8 %copy-start.15 = (bf16[256,1024]{1,0:T(8,128)(2,1)S(1)}, bf16[256,1024]{1,0:T(8,128)(2,1)}, u32[]{:S(2)}) copy-start(bf16[256,1024]{1,0:T(8,128)(2,1)} %param.33) | copy-start | bytes 1572868
  419.4 70.9 %copy-start.55 = (s32[256,2]{0,1:T(2,128)S(1)}, s32[256,2]{0,1:T(2,128)}, u32[]{:S(2)}) copy-start(s32[256,2]{0,1:T(2,128)} %get-tuple-element.20) | copy-start | bytes 6148
  419.4 65.0 %all-to-all-start.1 = ((bf16[2,320,1024]{2,0,1:T(2,128)(2,1)}), bf16[2,320,1024]{2,0,1:T(2,128)(2,1)S(1)}, u32[]{:S(2)}, u32[]{:S(2)}) async-start(bf16[2,320,1024]{2,0,1:T(2,128)(2,1)} %copy.104), calls=%async_computation.2 | async-start | bytes 2621440 | tf_op jit(solution)/shard_map/all_to_all | solution.py:142
  484.4 37.5 %all-to-all-start.3 = ((bf16[2,320,1024]{2,0,1:T(2,128)(2,1)}), bf16[2,320,1024]{2,0,1:T(2,128)(2,1)}, u32[]{:S(2)}, u32[]{:S(2)}) async-start(bf16[2,320,1024]{2,0,1:T(2,128)(2,1)} %copy.109), calls=%async_computation.5 | async-start | bytes 2621440 | tf_op jit(solution)/shard_map/all_to_all | solution.py:182
  489.0 149.4 %reduce-scatter.22.cloned.1.call-start = ((), (), s32[]{:S(2)}) async-start(), calls=%async_computation.23 | async-start | bytes 540672
  491.0 5.2 copy-start.32
  493.7 8.4 copy-start.48
  503.4 276.6 %reduce-scatter.20.cloned.1.call-start = ((), (), s32[]{:S(2)}) async-start(), calls=%async_computation.22 | async-start | bytes 4325376 | tf_op jit(solution)/shard_map/reduce_scatter | solution.py:263
  526.3 7.6 copy-start.7
  526.3 7.6 copy-start.41
  526.3 7.6 copy-start.50
  526.3 8.7 copy-start.54
  526.3 8.7 copy-start.16
  533.9 3.5 copy-start.31
  537.4 3.1 copy-start.8
  537.4 3.1 copy-start.36
  537.4 3.1 copy-start.39
  540.2 382.3 %reduce-scatter.18.cloned.1.call-start = ((), (), s32[]{:S(2)}) async-start(), calls=%async_computation.21 | async-start | bytes 4325376 | tf_op jit(solution)/shard_map/reduce_scatter | solution.py:262
  540.5 5.8 copy-start.5
  540.5 5.8 copy-start.34
  540.5 5.8 copy-start.43
  546.3 2.9 copy-start.21
  546.3 2.9 copy-start.29
  549.2 515.2 %reduce-scatter.16.cloned.1.call-start = ((), (), s32[]{:S(2)}) async-start(), calls=%async_computation.20 | async-start | bytes 4325376 | tf_op jit(solution)/shard_map/reduce_scatter | solution.py:261
  549.2 3.7 copy-start.3
  556.0 2.8 copy-start.13
  558.9 647.9 %reduce-scatter.14.cloned.1.call-start = ((), (), s32[]{:S(2)}) async-start(), calls=%async_computation.19 | async-start | bytes 4325376 | tf_op jit(solution)/shard_map/reduce_scatter | solution.py:260
  562.0 10.2 copy-start.62
  562.1 18.6 %slice-start = ((s8[5242880]{0:T(1024)(128)(4,1)}), s8[4194304]{0:T(1024)(128)(4,1)S(1)}, s32[]{:S(2)}) async-start(s8[5242880]{0:T(1024)(128)(4,1)} %bitcast.120), calls=%async_computation.24 | async-start | bytes 8388608
  572.2 8.4 slice-start.1
  572.2 8.4 copy-start.63
  580.6 5.7 copy-start.9
  580.6 6.5 copy-start.14
  586.3 2.4 copy-start.22
  586.3 2.4 copy-start.30
  587.9 2.7 copy-start.45
  587.9 40.9 %copy-start.52 = (f32[256]{0:T(256)S(1)}, f32[256]{0:T(256)}, u32[]{:S(2)}) copy-start(f32[256]{0:T(256)} %copy-done.51) | copy-start | bytes 3076
  587.9 618.9 %copy-start.1 = (bf16[2,704,1024]{2,1,0:T(8,128)(2,1)S(1)}, bf16[2,704,1024]{2,1,0:T(8,128)(2,1)}, u32[]{:S(2)}) copy-start(bf16[2,704,1024]{2,1,0:T(8,128)(2,1)} %param.32) | copy-start | bytes 8650756
  (18 other events, 24.3 us)
Sparse Core Ops, SparseCore 0:
  9.9 38.0 all-gather.8
  49.8 35.2 all-gather.10
  87.0 35.2 all-gather.12
  124.0 35.2 all-gather.14
  205.7 59.4 all-gather.16
  271.5 59.4 all-gather.18
  354.1 61.4 reduce-scatter.9
  419.2 61.4 reduce-scatter.11
  503.5 134.8 reduce-scatter.21
  641.2 138.7 reduce-scatter.19
  783.0 139.4 reduce-scatter.17
  925.3 139.0 reduce-scatter.15
  1067.3 139.4 reduce-scatter.13
where the time goes:
time: 1220 us; the launch traced here: 1210 us
  waiting for transfers between devices  838 us (69%)
  blocking collectives  136 us (11%)
  matrix products  122 us (10%)
  local copies, waits for them, and re-layouts  61.7 us (5%)
  other arithmetic  30.9 us (3%)
  between operations  15.2 us (1%)
    reduce_scatter x1, waiting for transfers between devices, shards(): lax.psum_scatter(query_wgrad, ('dp', 'expert'), scatter_dimension=0, tile...  142 us
    reduce_scatter x1, waiting for transfers between devices, shards(): lax.psum_scatter(value_wgrad, ('dp', 'expert'), scatter_dimension=0, tile...  142 us
    reduce_scatter x1, waiting for transfers between devices, shards(): lax.psum_scatter(key_wgrad, ('dp', 'expert'), scatter_dimension=0, tiled=...  142 us
    reduce_scatter x1, waiting for transfers between devices, shards(): lax.psum_scatter(out_wgrad, ('dp', 'expert'), scatter_dimension=0, tiled=...  140 us
    reduce_scatter x1, waiting for transfers between devices, shards(): lax.psum_scatter(rows_terms.astype(jnp.bfloat16), 'dp', scatter_dimension...  56.5 us
    all_gather x1, waiting for transfers between devices, shards(): grads_used = lax.all_gather(arrived_grad, 'dp', axis=1, tiled=True)  43.1 us
    reduce_scatter x1, waiting for transfers between devices, shards(): lax.psum_scatter(produced_terms.astype(jnp.bfloat16), 'dp', scatter_dimen...  42.2 us
    unnamed x1, blocking collectives  37 us
  transfers between devices with their start and end apart: 15, of which 13 were waited for; matrix products, arithmetic and copies ran while one was open for 15% of the time, Pallas kernels for 0%

commit v1 on v0

--- a/solution.py
+++ b/solution.py
@@ -1,6 +1,10 @@
+import functools
+
 import jax
 import jax.numpy as jnp
 from jax import lax
+from jax.experimental import pallas as pl
+from jax.experimental.pallas import tpu as pltpu
 from jax.sharding import PartitionSpec as P
 
 HEADS = 16
@@ -49,6 +53,133 @@
 
 def glu_apply(gate_part, up_part):
     return jax.nn.gelu(gate_part, approximate=True) * up_part
+
+
+MESH_ID = pl.DeviceIdType.MESH
+BF = jnp.bfloat16
+F32 = jnp.float32
+
+
+def places():
+    d = lax.axis_index("dp")
+    e = lax.axis_index("expert")
+    px, py = d % 2, d // 2
+    z, c = e // 2, e % 2
+    xn = py * 2 + (1 - px)
+    yn = (1 - py) * 2 + px
+    dn = (1 - py) * 2 + (1 - px)
+    return d, e, z, c, xn, yn, dn
+
+
+def greet(peers):
+    barrier = pltpu.get_barrier_semaphore()
+    for peer in peers:
+        pl.semaphore_signal(barrier, inc=1, device_id=peer, device_id_type=MESH_ID)
+    pl.semaphore_wait(barrier, len(peers))
+
+
+def push(src, dst, send, recv, peer):
+    copy = pltpu.make_async_remote_copy(
+        src_ref=src, dst_ref=dst, send_sem=send, recv_sem=recv, device_id=peer, device_id_type=MESH_ID
+    )
+    copy.start()
+    return copy
+
+
+def plus(*refs):
+    total = refs[0][...].astype(F32)
+    for ref in refs[1:]:
+        total = total + ref[...].astype(F32)
+    return total
+
+
+def scatter_kernel(widths, *refs):
+    n = len(widths)
+    parts, outs = refs[:n], refs[n : 2 * n]
+    scratch = refs[2 * n :]
+    sib, acc, got, fin, zin = (scratch[i * n : (i + 1) * n] for i in range(5))
+    send, recv = scratch[5 * n :]
+    d, e, z, c, xn, yn, dn = places()
+    sibling = (d, z * 2 + (1 - c))
+    to_x, to_y = (xn, e), (yn, e)
+    z_peers = [(d, ((z + k) % 4) * 2 + c) for k in (1, 2, 3)]
+    greet([sibling, to_x, to_y] + z_peers)
+    ops = []
+
+    def go(u, slot, src, dst, peer):
+        copy = push(src, dst, send.at[u, slot], recv.at[u, slot], peer)
+        ops.append(copy)
+        return copy
+
+    first = [go(u, 0, parts[u].at[1 - c], sib[u], sibling) for u in range(n)]
+    lo, hi = pl.ds(0, 2), pl.ds(2, 2)
+    stage = []
+    for u in range(n):
+        first[u].wait_recv()
+        acc[u][...] = plus(parts[u].at[c], sib[u]).astype(BF)
+        a, g = acc[u], got[u]
+        stage.append(
+            (
+                go(u, 1, a.at[dn, lo], g.at[0], to_x),
+                go(u, 2, a.at[dn, hi], g.at[1], to_y),
+                go(u, 3, a.at[xn, lo], g.at[2], to_x),
+                go(u, 4, a.at[yn, hi], g.at[3], to_y),
+            )
+        )
+    joined = []
+    for u in range(n):
+        a, g = acc[u], got[u]
+        stage[u][0].wait_recv()
+        a[yn, lo] = plus(a.at[yn, lo], g.at[0]).astype(BF)
+        one = go(u, 5, a.at[yn, lo], g.at[4], to_y)
+        stage[u][1].wait_recv()
+        a[xn, hi] = plus(a.at[xn, hi], g.at[1]).astype(BF)
+        two = go(u, 6, a.at[xn, hi], g.at[5], to_x)
+        joined.append((one, two))
+    last = []
+    for u in range(n):
+        a, g, f = acc[u], got[u], fin[u]
+        stage[u][2].wait_recv()
+        joined[u][0].wait_recv()
+        f[lo] = plus(a.at[d, lo], g.at[2], g.at[4]).astype(BF)
+        stage[u][3].wait_recv()
+        joined[u][1].wait_recv()
+        f[hi] = plus(a.at[d, hi], g.at[3], g.at[5]).astype(BF)
+        last.append(
+            [
+                go(u, 7 + k, f.at[(z + k + 1) % 4], zin[u].at[k], z_peers[k])
+                for k in range(3)
+            ]
+        )
+    for u in range(n):
+        for copy in last[u]:
+            copy.wait_recv()
+        outs[u][...] = plus(fin[u].at[z], zin[u].at[0], zin[u].at[1], zin[u].at[2])
+    for copy in ops:
+        copy.wait_send()
+
+
+def scatter_rows(parts):
+    widths = tuple(part.shape[-1] for part in parts)
+    n = len(widths)
+    space = pl.BlockSpec(memory_space=pltpu.VMEM)
+    scratch = []
+    for lead in ((4, 4), (4, 4), (6, 2), (4,), (3,)):
+        scratch += [pltpu.VMEM(lead + (32, w), BF) for w in widths]
+    return pl.pallas_call(
+        functools.partial(scatter_kernel, widths),
+        out_shape=[jax.ShapeDtypeStruct((32, w), F32) for w in widths],
+        in_specs=[space] * n,
+        out_specs=[space] * n,
+        scratch_shapes=scratch + [pltpu.SemaphoreType.DMA((n, 10))] * 2,
+        compiler_params=pltpu.CompilerParams(
+            collective_id=1, has_side_effects=True, vmem_limit_bytes=40 << 20
+        ),
+    )(*parts)
+
+
+def by_core(grad):
+    return grad.astype(BF).reshape(4, 4, 2, 32, grad.shape[-1]).transpose(2, 0, 1, 3, 4)
 
 
 def shards(
@@ -255,6 +386,24 @@
     unused_first, first_pull = jax.vjp(rms_scale, inputs, gain_onef)
     input_norm_grad, gain_one_grad = first_pull(normed_grad)
     token_grad = residual_grad + input_norm_grad
+    if lax.axis_size("dp") == 4 and lax.axis_size("expert") == 8:
+        small = jnp.concatenate([router_wgrad, gain_one_grad[:, None], gain_two_grad[:, None]], axis=1)
+        small = jnp.pad(small, ((0, 0), (0, 128 - small.shape[1])))
+        got = scatter_rows([by_core(g) for g in (out_wgrad, value_wgrad, query_wgrad, key_wgrad, small)])
+        return (
+            output,
+            token_grad,
+            got[4][:, EXPERTS],
+            got[2],
+            got[3],
+            got[1],
+            got[0],
+            got[4][:, EXPERTS + 1],
+            got[4][:, :EXPERTS],
+            gate_wgrad,
+            up_wgrad,
+            down_wgrad,
+        )
     summed = (
         lax.psum_scatter(gain_one_grad, ("dp", "expert"), scatter_dimension=0, tiled=True),
         lax.psum_scatter(query_wgrad, ("dp", "expert"), scatter_dimension=0, tiled=True),

time: 1220 us -> 664 us (0.54)
  waiting for transfers between devices: 838 us -> 258 us
  Pallas kernels: 0 us -> 58.6 us
  blocking collectives: 136 us -> 99.1 us
    reduce_scatter x4 -> x0, waiting for transfers between devices: 567 us -> none  [the longest x1 142 us: shards(): lax.psum_scatter(query_wgrad, ('dp', 'expert'), scatter_dimension=0, tile...]
    pallas_call x0 -> x1, Pallas kernels: none -> 58.6 us  [scatter_rows(): pl.pallas_call(functools.partial(scatter_kernel, widths), out_shape=[jax....]
    unnamed x1 -> x0, blocking collectives: 37 us -> none
    all_to_all x1, waiting for transfers between devices: 18.4 us -> 0.01 us  [shards(): lax.all_to_all(rows_grad, 'expert', split_axis=1, concat_axis=0, tiled=True)]
    reduce_scatter x1, waiting for transfers between devices: 42.2 us -> 55.3 us  [shards(): lax.psum_scatter(produced_terms.astype(jnp.bfloat16), 'dp', scatter_dimen...]
  transfers between devices with their start and end apart: 15 -> 10, of which waited for: 13 -> 8; matrix products, arithmetic and copies ran while one was open for 15% -> 17% of each run, Pallas kernels for 0% -> 0%
where the time goes in v1:
time: 664 us; the launch traced here: 654 us
  waiting for transfers between devices  258 us (39%)
  matrix products  113 us (17%)
  blocking collectives  99.1 us (15%)
  local copies, waits for them, and re-layouts  69.5 us (10%)
  Pallas kernels  58.6 us (9%)
  other arithmetic  30.5 us (5%)
  between operations  15.6 us (2%)
  starting transfers between devices  9.75 us (1%)
    pallas_call x1, Pallas kernels, scatter_rows(): pl.pallas_call(functools.partial(scatter_kernel, widths), out_shape=[jax....  58.6 us
    reduce_scatter x1, waiting for transfers between devices, shards(): lax.psum_scatter(produced_terms.astype(jnp.bfloat16), 'dp', scatter_dimen...  55.3 us
    reduce_scatter x1, waiting for transfers between devices, shards(): lax.psum_scatter(rows_terms.astype(jnp.bfloat16), 'dp', scatter_dimension...  53 us
    all_gather x1, waiting for transfers between devices, shards(): grads_used = lax.all_gather(arrived_grad, 'dp', axis=1, tiled=True)  43.2 us
    all_to_all x1, blocking collectives, shards(): lax.all_to_all(outgoing, 'expert', split_axis=0, concat_axis=1, tiled=True)  36.8 us
    all_to_all x1, blocking collectives, shards(): lax.all_to_all(outgoing_grad, 'expert', split_axis=0, concat_axis=1, tile...  35.7 us
    all_gather x1, waiting for transfers between devices, shards(): lax.all_gather(w_key, 'dp', axis=0, tiled=True)  33.6 us
    all_gather x1, waiting for transfers between devices, shards(): lax.all_gather(w_query, 'dp', axis=0, tiled=True)  31.8 us
  transfers between devices with their start and end apart: 10, of which 8 were waited for; matrix products, arithmetic and copies ran while one was open for 17% of the time, Pallas kernels for 0%

profile of v1, /device:TPU:0, one launch (start us, length us, event | category | flops | bytes accessed | tf_op | source)
XLA Modules:
  0.0 654.2 jit_solution(13521685281407107479)
XLA Ops:
  11.3 9.5 %all-gather = bf16[4,1,256]{2,1,0:T(2,128)(2,1)S(1)} all-gather(bf16[1,1,256]{2,1,0:T(2,128)(2,1)S(1)} %reshape.470), channel_id=1, replica_groups=mesh['dp'=4,'expert'=8] {'dp'}, dimensions={0}, use_global_device_ids=true | all-gather | bytes 2560 | tf_op jit(solution)/shard_map/all_gather | solution.py:207
  23.3 1.2 convert_element_type.120
  25.2 8.1 %all-gather.1 = bf16[4,1,256]{2,1,0:T(2,128)(2,1)S(1)} all-gather(bf16[1,1,256]{2,1,0:T(2,128)(2,1)S(1)} %reshape.472), channel_id=1, replica_groups=mesh['dp'=4,'expert'=8] {'dp'}, dimensions={0}, use_global_device_ids=true | all-gather | bytes 2560 | tf_op jit(solution)/shard_map/all_gather | solution.py:212
  33.3 1.3 compare_select_fusion.3
  34.9 2.6 scatter_custom_fusion
  39.0 1.5 fusion.35
  40.5 7.4 %all-gather.9.cloned.1.call-done = bf16[1024,1024]{1,0:T(8,128)(2,1)} async-done(((bf16[256,1024]{1,0:T(8,128)(2,1)}), bf16[1024,1024]{1,0:T(8,128)(2,1)}) %all-gather.9.cloned.1.call-update) | async-done | bytes 2097168 | tf_op jit(solution)/shard_map/all_gather | solution.py:210
  47.9 3.3 convolution_convert_fusion.6
  51.3 2.0 copy.119
  53.3 31.8 %all-gather.11.cloned.1.call-done = bf16[1024,1024]{1,0:T(8,128)(2,1)} async-done(((bf16[256,1024]{1,0:T(8,128)(2,1)}), bf16[1024,1024]{1,0:T(8,128)(2,1)}) %all-gather.11.cloned.1.call-update) | async-done | bytes 2097168 | tf_op jit(solution)/shard_map/all_gather | solution.py:208
  85.1 3.6 fusion.61
  88.7 33.6 %all-gather.13.cloned.1.call-done = bf16[1024,1024]{1,0:T(8,128)(2,1)} async-done(((bf16[256,1024]{1,0:T(8,128)(2,1)}), bf16[1024,1024]{1,0:T(8,128)(2,1)}) %all-gather.13.cloned.1.call-update) | async-done | bytes 2097168 | tf_op jit(solution)/shard_map/all_gather | solution.py:209
  122.3 2.7 fusion.59
  128.5 1.2 copy-done.6
  129.7 1.9 fusion.19
  131.6 27.7 %all-gather.15.cloned.1.call-done = bf16[1024,1024]{1,0:T(8,128)(2,1)} async-done(((bf16[256,1024]{1,0:T(8,128)(2,1)}), bf16[1024,1024]{1,0:T(8,128)(2,1)}) %all-gather.15.cloned.1.call-update) | async-done | bytes 2097168 | tf_op jit(solution)/shard_map/all_gather | solution.py:211
  159.4 2.6 multiply_reduce_fusion.5
  164.0 3.5 gather_fusion
  167.5 36.8 %all_to_all.66 = bf16[16,40,1024]{2,1,0:T(8,128)(2,1)S(1)} all-to-all(bf16[16,40,1024]{2,1,0:T(8,128)(2,1)} %bitcast.121), channel_id=1, replica_groups=mesh['dp'=4,'expert'=8] {'expert'}, dimensions={0} | all-to-all | bytes 2621440 | tf_op jit(solution)/shard_map/all_to_all | solution.py:264
  205.6 3.0 mul.414
  208.5 3.6 mul.415
  212.2 9.0 %all_gather.33 = bf16[1024,16]{0,1:T(8,128)(2,1)S(1)} all-gather(bf16[256,16]{0,1:T(8,128)(2,1)} %param.29), channel_id=1, replica_groups=mesh['dp'=4,'expert'=8] {'dp'}, dimensions={0}, use_global_device_ids=true | all-gather | bytes 40960 | tf_op jit(solution)/shard_map/all_gather | solution.py:213
  222.1 1.5 copy.123
  223.6 1.6 div.80
  225.2 1.8 multiply_convert_fusion.3
  227.0 1.3 concatenate.28
  228.2 5.8 gather_fusion.2
  234.1 35.7 %all_to_all.67 = bf16[16,40,1024]{2,1,0:T(8,128)(2,1)S(1)} all-to-all(bf16[16,40,1024]{2,1,0:T(8,128)(2,1)} %bitcast.122), channel_id=1, replica_groups=mesh['dp'=4,'expert'=8] {'expert'}, dimensions={0} | all-to-all | bytes 2621440 | tf_op jit(solution)/shard_map/all_to_all | solution.py:292
  271.1 10.3 %fusion.65 = f32[2,1280,704]{1,2,0:T(8,128)} fusion(bf16[2,1280,1024]{2,1,0:T(8,128)(2,1)} %all-gather.17.cloned.1.call-done, bf16[2,1024,704]{1,2,0:T(8,128)(2,1)} %param.30), kind=kOutput, calls=%fused_computation.149 | convolution fusion | flops 3690987520 | bytes 15335424 | tf_op jit(solution)/shard_map/erd,edf->erf/dot_general | solution.py:266
  281.4 6.0 fusion.66
  287.4 43.2 %all-gather.19.cloned.1.call-done = bf16[2,1280,1024]{2,1,0:T(8,128)(2,1)} async-done(((bf16[2,320,1024]{2,1,0:T(8,128)(2,1)}), bf16[2,1280,1024]{2,1,0:T(8,128)(2,1)}) %all-gather.19.cloned.1.call-update) | async-done | bytes 5242896 | tf_op jit(solution)/shard_map/all_gather | solution.py:293
  330.6 15.5 %multiply_convert_fusion = (bf16[2,1280,704]{1,2,0:T(8,128)(2,1)S(1)}, bf16[2,1280,704]{1,2,0:T(8,128)(2,1)}, bf16[2,1280,704]{1,2,0:T(8,128)(2,1)}) fusion(f32[2,1280,704]{1,2,0:T(8,128)} %fusion.65, f32[2,1280,704]{1,2,0:T(8,128)} %fusion.66, bf16[2,1280,1024]{2,1,0:T(8,128)(2,1)} %all-gather.19.cloned.1.call-done, bf16[2,704,1024]{2,1,0:T(8,128)(2,1)S(1)} %copy-done), kind=kOutput, calls=%fused_computation.15 | convolution fusion | flops 3737845760 | bytes 33357824 | tf_op jit(solution)/shard_map/erd,efd->erf/dot_general | solution.py:295
  346.1 10.2 %fusion.67 = f32[2,1280,1024]{2,1,0:T(8,128)} fusion(bf16[2,1280,704]{1,2,0:T(8,128)(2,1)} %get-tuple-element.93, bf16[2,1024,704]{1,2,0:T(8,128)(2,1)S(1)} %copy-done.69), kind=kOutput, calls=%fused_computation.151 | convolution fusion | flops 3690987520 | bytes 16973824 | tf_op jit(solution)/shard_map/erf,edf->erd/dot_general | solution.py:305
  356.3 8.5 %add_convert_fusion = bf16[2,1280,1024]{2,1,0:T(8,128)(2,1)} fusion(f32[2,1280,1024]{2,1,0:T(8,128)} %fusion.67, bf16[2,1280,704]{1,2,0:T(8,128)(2,1)S(1)} %get-tuple-element.92, bf16[2,1024,704]{1,2,0:T(8,128)(2,1)S(1)} %copy-done.71), kind=kOutput, calls=%fused_computation.5 | convolution fusion | flops 3696230400 | bytes 22216704 | tf_op jit(solution)/shard_map/erf,edf->erd/dot_general | solution.py:306
  364.9 8.5 %convolution_convert_fusion = bf16[2,1280,1024]{2,1,0:T(8,128)(2,1)} fusion(bf16[2,1280,704]{1,2,0:T(8,128)(2,1)} %get-tuple-element.94, bf16[2,704,1024]{2,1,0:T(8,128)(2,1)S(1)} %copy-done), kind=kOutput, calls=%fused_computation.18 | convolution fusion | flops 3693608960 | bytes 11730944 | tf_op jit(solution)/shard_map/erf,efd->erd/dot_general | solution.py:269
  373.4 53.0 %reduce-scatter.5.cloned.1.call-done = bf16[2,320,1024]{2,1,0:T(8,128)(2,1)} async-done(((bf16[2,1280,1024]{2,1,0:T(8,128)(2,1)}), bf16[2,320,1024]{2,1,0:T(8,128)(2,1)}) %reduce-scatter.5.cloned.1.call-update) | async-done | bytes 1310736 | tf_op jit(solution)/shard_map/reduce_scatter | solution.py:310
  426.4 3.7 copy.131
  430.2 4.6 all-to-all-start.3
  436.2 55.3 %reduce-scatter.3.cloned.1.call-done = bf16[2,320,1024]{2,1,0:T(8,128)(2,1)} async-done(((bf16[2,1280,1024]{2,1,0:T(8,128)(2,1)}), bf16[2,320,1024]{2,1,0:T(8,128)(2,1)}) %reduce-scatter.3.cloned.1.call-update) | async-done | bytes 1310736 | tf_op jit(solution)/shard_map/reduce_scatter | solution.py:270
  491.5 3.8 copy.126
  495.2 4.8 all-to-all-start.1
  500.1 10.1 %fusion.70 = f32[2,1024,704]{1,2,0:T(8,128)} fusion(bf16[2,1280,704]{1,2,0:T(8,128)(2,1)} %get-tuple-element.93, bf16[2,1280,1024]{2,1,0:T(8,128)(2,1)} %all-gather.17.cloned.1.call-done), kind=kOutput, calls=%fused_computation.154 | convolution fusion | flops 3690987520 | bytes 14614528 | tf_op jit(solution)/shard_map/erd,erf->edf/dot_general | solution.py:303
  510.2 8.4 %fusion.71 = f32[2,1024,704]{1,2,0:T(8,128)} fusion(bf16[2,1280,704]{1,2,0:T(8,128)(2,1)S(1)} %copy-done.73, bf16[2,1280,1024]{2,1,0:T(8,128)(2,1)} %all-gather.17.cloned.1.call-done), kind=kOutput, calls=%fused_computation.155 | convolution fusion | flops 3690987520 | bytes 14614528 | tf_op jit(solution)/shard_map/erd,erf->edf/dot_general | solution.py:304
  518.6 5.7 fusion.69
  524.6 2.1 gather_fusion.3
  526.7 2.3 reshape.469
  529.0 3.3 all-to-all-done.1
  532.3 1.7 copy.127
  534.0 2.1 gather_fusion.1
  536.1 2.4 reshape.468
  538.5 6.5 multiply_reduce_fusion.1
  545.2 4.1 reduce_sum.141
  553.2 3.6 multiply_reduce_fusion
  566.6 1.9 fusion.23
  568.5 1.5 copy.161
  570.0 1.5 copy.160
  571.6 1.5 copy.159
  573.1 1.5 copy.158
  575.0 1.6 copy-done.2
  576.5 1.6 copy-done.3
  578.1 1.6 copy-done.4
  579.7 1.6 copy-done.5
  581.3 58.6 %shard_map.256 = (f32[32,1024]{1,0:T(8,128)S(1)}, f32[32,1024]{1,0:T(8,128)S(1)}, f32[32,1024]{1,0:T(8,128)S(1)}, f32[32,1024]{1,0:T(8,128)S(1)}, f32[32,128]{1,0:T(8,128)S(1)}) custom-call(bf16[2,4,4,32,1024]{4,3,2,1,0:T(8,128)(2,1)S(1)} %bitcast.104, bf16[2,4,4,32,1024]{4,3,2,1,0:T(8,128)(2,1)S(1)} %bitcast.105, ...), custom_call_target="tpu_custom_call" | custom-call | tf_op jit(solution)/shard_map/pallas_call | solution.py:169
  641.3 3.0 fusion.25
  (238 shorter events, 37.4 us)
Async XLA Ops:
  7.2 323.4 %copy-start = (bf16[2,704,1024]{2,1,0:T(8,128)(2,1)S(1)}, bf16[2,704,1024]{2,1,0:T(8,128)(2,1)}, u32[]{:S(2)}) copy-start(bf16[2,704,1024]{2,1,0:T(8,128)(2,1)} %param.32) | copy-start | bytes 8650756
  7.2 40.7 %all-gather.9.cloned.1.call-start = ((), (), s32[]{:S(2)}) async-start(), calls=%async_computation.6 | async-start | bytes 2621440 | tf_op jit(solution)/shard_map/all_gather | solution.py:210
  7.9 77.2 %copy-start.8 = (bf16[256,1024]{1,0:T(8,128)(2,1)S(1)}, bf16[256,1024]{1,0:T(8,128)(2,1)}, u32[]{:S(2)}) copy-start(bf16[256,1024]{1,0:T(8,128)(2,1)} %param.17) | copy-start | bytes 1572868
  7.9 77.2 %all-gather.11.cloned.1.call-start = ((), (), s32[]{:S(2)}) async-start(), calls=%async_computation.7 | async-start | bytes 2621440 | tf_op jit(solution)/shard_map/all_gather | solution.py:208
  8.7 113.6 %all-gather.13.cloned.1.call-start = ((), (), s32[]{:S(2)}) async-start(), calls=%async_computation.8 | async-start | bytes 2621440 | tf_op jit(solution)/shard_map/all_gather | solution.py:209
  9.4 149.9 %all-gather.15.cloned.1.call-start = ((), (), s32[]{:S(2)}) async-start(), calls=%async_computation.9 | async-start | bytes 2621440 | tf_op jit(solution)/shard_map/all_gather | solution.py:211
  10.0 261.0 %all-gather.17.cloned.1.call-start = ((), (), s32[]{:S(2)}) async-start(), calls=%async_computation.10 | async-start | bytes 6553600 | tf_op jit(solution)/shard_map/all_gather | solution.py:265
  20.8 101.5 %copy-start.38 = (f32[4,1,256]{2,1,0:T(1,128)}, f32[4,1,256]{2,1,0:T(1,128)S(1)}, u32[]{:S(2)}) copy-start(f32[4,1,256]{2,1,0:T(1,128)S(1)} %convert_element_type.154) | copy-start | bytes 12292
  22.0 3.1 copy-start.62
  22.1 100.3 %copy-start.51 = (f32[256]{0:T(256)}, f32[256]{0:T(256)S(1)}, u32[]{:S(2)}) copy-start(f32[256]{0:T(256)S(1)} %fusion.46) | copy-start | bytes 3076
  33.3 128.7 %copy-start.49 = (f32[4,1,256]{2,1,0:T(1,128)}, f32[4,1,256]{2,1,0:T(1,128)S(1)}, u32[]{:S(2)}) copy-start(f32[4,1,256]{2,1,0:T(1,128)S(1)} %convert_element_type.155) | copy-start | bytes 12292
  122.3 2.7 copy-start.27
  127.7 2.0 copy-start.6
  127.7 3.9 copy-start.40
  127.7 2.0 copy-start.35
  162.0 5.5 copy-start.64
  162.0 5.5 copy-start.60
  205.5 15.7 %copy-start.18 = (bf16[256,1024]{1,0:T(8,128)(2,1)S(1)}, bf16[256,1024]{1,0:T(8,128)(2,1)}, u32[]{:S(2)}) copy-start(bf16[256,1024]{1,0:T(8,128)(2,1)} %copy-done.17) | copy-start | bytes 1572868
  205.5 15.9 %copy-start.55 = (s32[256,2]{0,1:T(2,128)S(1)}, s32[256,2]{0,1:T(2,128)}, u32[]{:S(2)}) copy-start(s32[256,2]{0,1:T(2,128)} %param.21) | copy-start | bytes 6148
  205.5 125.0 %all-gather.19.cloned.1.call-start = ((), (), s32[]{:S(2)}) async-start(), calls=%async_computation.12 | async-start | bytes 6553600 | tf_op jit(solution)/shard_map/all_gather | solution.py:293
  212.2 16.1 %copy-start.57 = (s32[1024]{0:T(1024)S(1)}, s32[1024]{0:T(1024)}, u32[]{:S(2)}) copy-start(s32[1024]{0:T(1024)} %get-tuple-element.122) | copy-start | bytes 12292
  221.4 12.6 %copy-start.45 = (f32[256,2]{0,1:T(2,128)}, f32[256,2]{0,1:T(2,128)S(1)}, u32[]{:S(2)}) copy-start(f32[256,2]{0,1:T(2,128)S(1)} %select_reduce_fusion.2) | copy-start | bytes 6148
  221.5 12.6 %copy-start.53 = (f32[256]{0:T(256)}, f32[256]{0:T(256)S(1)}, u32[]{:S(2)}) copy-start(f32[256]{0:T(256)S(1)} %reduce_max.19) | copy-start | bytes 3076
  221.5 12.6 %copy-start.58 = (f32[256]{0:T(256)}, f32[256]{0:T(256)S(1)}, u32[]{:S(2)}) copy-start(f32[256]{0:T(256)S(1)} %fusion.45) | copy-start | bytes 3076
  271.0 155.5 %reduce-scatter.5.cloned.1.call-start = ((), (), s32[]{:S(2)}) async-start(), calls=%async_computation.13 | async-start | bytes 6553600 | tf_op jit(solution)/shard_map/reduce_scatter | solution.py:310
  271.0 10.3 %copy-start.68 = (bf16[2,1280,1024]{2,1,0:T(8,128)(2,1)S(1)}, bf16[2,1280,1024]{2,1,0:T(8,128)(2,1)}, u32[]{:S(2)}) copy-start(bf16[2,1280,1024]{2,1,0:T(8,128)(2,1)} %all-gather.17.cloned.1.call-done) | copy-start | bytes 15728644
  271.1 10.3 %copy-start.70 = (bf16[2,1024,704]{1,2,0:T(8,128)(2,1)S(1)}, bf16[2,1024,704]{1,2,0:T(8,128)(2,1)}, u32[]{:S(2)}) copy-start(bf16[2,1024,704]{1,2,0:T(8,128)(2,1)} %param.31) | copy-start | bytes 8650756
  330.6 15.5 %copy-start.69 = (bf16[2,1024,704]{1,2,0:T(8,128)(2,1)S(1)}, bf16[2,1024,704]{1,2,0:T(8,128)(2,1)}, u32[]{:S(2)}) copy-start(bf16[2,1024,704]{1,2,0:T(8,128)(2,1)} %param.30) | copy-start | bytes 8650756
  346.1 10.3 %copy-start.72 = (bf16[2,1280,704]{1,2,0:T(8,128)(2,1)}, bf16[2,1280,704]{1,2,0:T(8,128)(2,1)S(1)}, u32[]{:S(2)}) copy-start(bf16[2,1280,704]{1,2,0:T(8,128)(2,1)S(1)} %get-tuple-element.92) | copy-start | bytes 10813444
  346.1 10.2 %copy-start.71 = (bf16[2,1024,704]{1,2,0:T(8,128)(2,1)S(1)}, bf16[2,1024,704]{1,2,0:T(8,128)(2,1)}, u32[]{:S(2)}) copy-start(bf16[2,1024,704]{1,2,0:T(8,128)(2,1)} %param.31) | copy-start | bytes 8650756
  364.8 126.6 %reduce-scatter.3.cloned.1.call-start = ((), (), s32[]{:S(2)}) async-start(), calls=%async_computation.11 | async-start | bytes 6553600 | tf_op jit(solution)/shard_map/reduce_scatter | solution.py:270
  373.4 61.4 %copy-start.19 = (bf16[256,1024]{1,0:T(8,128)(2,1)S(1)}, bf16[256,1024]{1,0:T(8,128)(2,1)}, u32[]{:S(2)}) copy-start(bf16[256,1024]{1,0:T(8,128)(2,1)} %param.33) | copy-start | bytes 1572868
  373.4 62.4 %copy-start.67 = (s32[256,2]{0,1:T(2,128)S(1)}, s32[256,2]{0,1:T(2,128)}, u32[]{:S(2)}) copy-start(s32[256,2]{0,1:T(2,128)} %get-tuple-element.90) | copy-start | bytes 6148
  373.4 62.7 %copy-start.41 = (f32[16,256]{1,0:T(8,128)S(1)}, f32[16,256]{1,0:T(8,128)}, u32[]{:S(2)}) copy-start(f32[16,256]{1,0:T(8,128)} %copy-done.40) | copy-start | bytes 49156
  373.4 62.7 %copy-start.48 = (f32[16,256]{1,0:T(8,128)S(1)}, f32[16,256]{1,0:T(8,128)}, u32[]{:S(2)}) copy-start(f32[16,256]{1,0:T(8,128)} %copy-done.47) | copy-start | bytes 49156
  430.2 65.1 %all-to-all-start.3 = ((bf16[2,320,1024]{2,0,1:T(2,128)(2,1)}), bf16[2,320,1024]{2,0,1:T(2,128)(2,1)S(1)}, u32[]{:S(2)}, u32[]{:S(2)}) async-start(bf16[2,320,1024]{2,0,1:T(2,128)(2,1)} %copy.131), calls=%async_computation.5 | async-start | bytes 2621440 | tf_op jit(solution)/shard_map/all_to_all | solution.py:313
  495.2 37.1 %all-to-all-start.1 = ((bf16[2,320,1024]{2,0,1:T(2,128)(2,1)}), bf16[2,320,1024]{2,0,1:T(2,128)(2,1)}, u32[]{:S(2)}, u32[]{:S(2)}) async-start(bf16[2,320,1024]{2,0,1:T(2,128)(2,1)} %copy.126), calls=%async_computation.2 | async-start | bytes 2621440 | tf_op jit(solution)/shard_map/all_to_all | solution.py:273
  500.1 10.2 %copy-start.73 = (bf16[2,1280,704]{1,2,0:T(8,128)(2,1)S(1)}, bf16[2,1280,704]{1,2,0:T(8,128)(2,1)}, u32[]{:S(2)}) copy-start(bf16[2,1280,704]{1,2,0:T(8,128)(2,1)} %copy-done.72) | copy-start | bytes 10813444
  500.1 18.5 %slice-start = ((s8[5242880]{0:T(1024)(128)(4,1)}), s8[4194304]{0:T(1024)(128)(4,1)S(1)}, s32[]{:S(2)}) async-start(s8[5242880]{0:T(1024)(128)(4,1)} %bitcast.150), calls=%async_computation.14 | async-start | bytes 8388608
  510.2 8.4 %slice-start.1 = ((s8[5242880]{0:T(1024)(128)(4,1)}), s8[1048576]{0:T(1024)(128)(4,1)S(1)}, s32[]{:S(2)}) async-start(s8[5242880]{0:T(1024)(128)(4,1)} %bitcast.150), calls=%async_computation.15 | async-start | bytes 2097152
  510.2 8.4 %copy-start.74 = (bf16[2,1280,704]{1,2,0:T(8,128)(2,1)S(1)}, bf16[2,1280,704]{1,2,0:T(8,128)(2,1)}, u32[]{:S(2)}) copy-start(bf16[2,1280,704]{1,2,0:T(8,128)(2,1)} %get-tuple-element.94) | copy-start | bytes 10813444
  534.0 4.5 copy-start.37
  536.1 9.0 %copy-start.46 = (f32[256,2]{0,1:T(2,128)S(1)}, f32[256,2]{0,1:T(2,128)}, u32[]{:S(2)}) copy-start(f32[256,2]{0,1:T(2,128)} %copy-done.45) | copy-start | bytes 6148
  536.1 9.0 %copy-start.54 = (f32[256]{0:T(256)S(1)}, f32[256]{0:T(256)}, u32[]{:S(2)}) copy-start(f32[256]{0:T(256)} %copy-done.53) | copy-start | bytes 3076
  536.1 9.0 %copy-start.59 = (f32[256]{0:T(256)S(1)}, f32[256]{0:T(256)}, u32[]{:S(2)}) copy-start(f32[256]{0:T(256)} %copy-done.58) | copy-start | bytes 3076
  536.1 9.1 %copy-start.56 = (s32[256,2]{0,1:T(2,128)S(1)}, s32[256,2]{0,1:T(2,128)}, u32[]{:S(2)}) copy-start(s32[256,2]{0,1:T(2,128)} %param.21) | copy-start | bytes 6148
  538.5 10.8 %copy-start.11 = (f32[256,1024]{1,0:T(8,128)S(1)}, f32[256,1024]{1,0:T(8,128)}, u32[]{:S(2)}) copy-start(f32[256,1024]{1,0:T(8,128)} %copy-done.10) | copy-start | bytes 3145732
  538.5 10.8 %copy-start.50 = (f32[4,1,256]{2,1,0:T(1,128)S(1)}, f32[4,1,256]{2,1,0:T(1,128)}, u32[]{:S(2)}) copy-start(f32[4,1,256]{2,1,0:T(1,128)} %copy-done.49) | copy-start | bytes 12292
  538.5 10.8 %copy-start.61 = (f32[256]{0:T(256)S(1)}, f32[256]{0:T(256)}, u32[]{:S(2)}) copy-start(f32[256]{0:T(256)} %copy-done.60) | copy-start | bytes 3076
  545.0 5.4 copy-start.65
  545.0 5.4 copy-start.20
  545.2 6.5 %copy-start.43 = (bf16[256,16]{0,1:T(8,128)(2,1)}, bf16[256,16]{0,1:T(8,128)(2,1)S(1)}, u32[]{:S(2)}) copy-start(bf16[256,16]{0,1:T(8,128)(2,1)S(1)} %select_reduce_fusion.1) | copy-start | bytes 24580
  549.3 2.4 copy-start.15
  551.8 5.0 copy-start.12
  552.8 4.1 copy-start.25
  553.2 3.7 copy-start.7
  559.6 1.9 copy-start.9
  559.6 1.9 copy-start.39
  559.6 1.9 copy-start.52
  562.8 2.0 copy-start.14
  563.7 1.9 copy-start.16
  566.6 1.9 copy-start.63
  571.6 3.1 copy-start.66
  581.3 65.6 %copy-start.1 = (bf16[2,704,1024]{2,1,0:T(8,128)(2,1)S(1)}, bf16[2,704,1024]{2,1,0:T(8,128)(2,1)}, u32[]{:S(2)}) copy-start(bf16[2,704,1024]{2,1,0:T(8,128)(2,1)} %param.32) | copy-start | bytes 8650756
  (23 other events, 31.9 us)
Sparse Core Ops, SparseCore 0:
  9.9 38.0 all-gather.8
  49.8 35.2 all-gather.10
  87.0 35.2 all-gather.12
  124.0 35.2 all-gather.14
  205.6 59.4 all-gather.16
  271.1 59.4 all-gather.18
  365.0 61.4 reduce-scatter.4
  430.0 61.4 reduce-scatter.2
